TPU v7x, 128 devices: a whole 4x4x4 slice. The times are simulated.
128 devices in a mesh: ctx: 32 (over y_hi, x, z), fsdp: 4 (over y_lo, core).
Axes of the slice: x: 4, y: 4 (y_hi: 2, y_lo: 2; y = y_hi * 2 + y_lo), z: 4, core: 2. Of those that a mesh axis runs over, the one named last changes fastest.
Arguments:
- layer_input: bfloat16 [4, 4096, 1024], P('fsdp', 'ctx'), may hold values from -6 to 6
- cotangent: bfloat16 [4, 4096, 1024], P('fsdp', 'ctx'), may hold values from -6 to 6
- block_order: int32 [4, 64], P('fsdp'), may hold values from 0 to 63, as said below
- query_weight: bfloat16 [1024, 2048], P('fsdp'), may hold values from -0.1875 to 0.1875
- key_projection: bfloat16 [1024, 1024], P('fsdp'), may hold values from -0.1875 to 0.1875
- value_projection: bfloat16 [1024, 1024], P('fsdp'), may hold values from -0.1875 to 0.1875
- output_weight: bfloat16 [2048, 1024], P('fsdp'), may hold values from -0.75 to 0.75
- gate_weight: bfloat16 [1024, 3072], P('fsdp'), may hold values from -0.1875 to 0.1875
- up_weight: bfloat16 [1024, 3072], P('fsdp'), may hold values from -0.1875 to 0.1875
- down_weight: bfloat16 [3072, 1024], P('fsdp'), may hold values from -0.109375 to 0.109375
- first_gain: float32 [1024], replicated, may hold values from 0.5 to 1.5
- second_gain: float32 [1024], replicated, may hold values from 0.5 to 1.5
- query_gain: float32 [128], replicated, may hold values from 0.25 to 1.75
- key_norm_gain: float32 [128], replicated, may hold values from 0.25 to 1.75
Outputs:
- layer_output: bfloat16 [4, 4096, 1024], P('fsdp', 'ctx')
- input_gradient: float32 [4, 4096, 1024], P('fsdp', 'ctx')
- query_weight_gradient: float32 [1024, 2048], P('fsdp')
- key_weight_gradient: float32 [1024, 1024], P('fsdp')
- value_weight_gradient: float32 [1024, 1024], P('fsdp')
- output_weight_gradient: float32 [2048, 1024], P('fsdp')
- gate_weight_gradient: float32 [1024, 3072], P('fsdp')
- up_weight_gradient: float32 [1024, 3072], P('fsdp')
- down_weight_gradient: float32 [3072, 1024], P('fsdp')
- first_gain_gradient: float32 [1024], P('fsdp')
- second_gain_gradient: float32 [1024], P('fsdp')
- query_gain_gradient: float32 [128], P('fsdp')
- key_gain_gradient: float32 [128], P('fsdp')
Inputs may be any that keep to these rules, and one draw needn't show every extreme that they name: Each row of block_order names every block of 64 positions of its sequence exactly once; the two blocks of rows 2 c and 2 c + 1 are mirrored, block b together with block 2 * 32 - 1 - b, in either order.
All inputs are finite; a program needn't handle non-finite values.
Results may differ from a plain program's by a relative error of at most 0.034.
Values may be sent and summed in bfloat16 or wider, within the bound.
No kernel may reach another device: no remote copies, remote signals or barrier semaphores. Data moves between devices by JAX's collectives and lax.ppermute only.
A program may use at most 320 MiB of HBM per device.

v0:
```python
import math
import jax
import jax.numpy as jnp
from jax import lax
from jax.sharding import PartitionSpec as P

HQ = 16
KEY_VALUE_HEADS = 8
HEAD_SIZE = 128
CTX = ("yh", "x", "z")
FSDP = ("yl", "c")
EPSILON = 1e-06
THETA = 1000000.0
MASKED = -1e30


def rms_apply(values, norm_gain):
    row_scale = lax.rsqrt(jnp.mean(values * values, axis=-1, keepdims=True) + EPSILON)
    normed = values * row_scale
    return (normed * norm_gain, normed, row_scale)


def root_mean_square_backward(gradient, normed, row_scale, norm_gain):
    normed_grad = gradient * norm_gain
    return row_scale * (
        normed_grad - normed * jnp.mean(normed_grad * normed, axis=-1, keepdims=True)
    )


def rope_tables(positions, head_width):
    half_width = head_width // 2
    inverse_freq = jnp.power(THETA, -2.0 * jnp.arange(half_width, dtype=jnp.float32) / head_width)
    angles = positions.astype(jnp.float32)[:, None] * inverse_freq[None, :]
    return (jnp.cos(angles)[:, None, :], jnp.sin(angles)[:, None, :])


def rotary_apply(values, cosine_table, sine_values_table):
    half_width = values.shape[-1] // 2
    front_half = values[..., :half_width]
    back_half = values[..., half_width:]
    return jnp.concatenate(
        [
            front_half * cosine_table - back_half * sine_values_table,
            back_half * cosine_table + front_half * sine_values_table,
        ],
        axis=-1,
    )


def rotary_backward(gradient, cosine_table, sine_values_table):
    half_width = gradient.shape[-1] // 2
    front_half = gradient[..., :half_width]
    back_half = gradient[..., half_width:]
    return jnp.concatenate(
        [
            front_half * cosine_table + back_half * sine_values_table,
            back_half * cosine_table - front_half * sine_values_table,
        ],
        axis=-1,
    )


def left_dot(left_side, right_side):
    return lax.dot_general(
        left_side, right_side, (((0,), (0,)), ((), ())), preferred_element_type=jnp.float32
    )


def right_dot(left_side, right_side):
    return lax.dot_general(
        left_side, right_side, (((1,), (1,)), ((), ())), preferred_element_type=jnp.float32
    )


def gather_fsdp(values):
    across = lax.all_gather(values, "yl", axis=0, tiled=False)
    both = lax.all_gather(across, "c", axis=1, tiled=False)
    return both.reshape((-1,) + values.shape[1:])


def reduce_ctx(shards):
    flat = jnp.concatenate([s.astype(jnp.bfloat16).reshape(-1) for s in shards])
    lanes = 128
    step = 256 * lanes
    padded = -(-flat.shape[0] // step) * step
    flat = jnp.pad(flat, (0, padded - flat.shape[0])).reshape(padded // lanes, lanes)
    part = lax.psum_scatter(flat, "z", scatter_dimension=0, tiled=True)
    part = lax.psum_scatter(part, "x", scatter_dimension=0, tiled=True)
    part = lax.psum(part, "yh")
    part = lax.all_gather(part, "x", axis=0, tiled=True)
    full = lax.all_gather(part, "z", axis=0, tiled=True).reshape(-1)
    out = []
    at = 0
    for s in shards:
        out.append(full[at : at + s.size].reshape(s.shape).astype(jnp.float32))
        at += s.size
    return tuple(out)


def on_device(
    layer_input,
    cotangent,
    block_order,
    query_weight,
    key_projection,
    value_projection,
    output_weight,
    gate_weight,
    up_weight,
    down_weight,
    first_gain,
    second_gain,
    query_gain,
    key_norm_gain,
):
    local_rows = layer_input.shape[1]
    block_rows = local_rows // 2
    ctx_size = lax.axis_size(CTX)
    halves = ctx_size // HQ
    half_devices = ctx_size // halves
    order_row = block_order[0]
    device_place = lax.axis_index(CTX)
    my_half = device_place // half_devices
    all_positions = (
        order_row[:, None] * block_rows + jnp.arange(block_rows, dtype=jnp.int32)[None, :]
    ).reshape(-1)
    own_positions = lax.dynamic_slice_in_dim(all_positions, device_place * local_rows, local_rows)
    cosine_table, sine_values_table = rope_tables(own_positions, HEAD_SIZE)
    scale_factor = 1.0 / math.sqrt(HEAD_SIZE)
    half_rows = half_devices * local_rows
    query_positions = lax.dynamic_slice_in_dim(all_positions, my_half * half_rows, half_rows)
    allowed = all_positions[None, :] <= query_positions[:, None]
    half_select = (jnp.arange(halves, dtype=jnp.int32) == my_half)[:, None, None, None]

    def to_heads(per_head):
        by_head = jnp.transpose(per_head, (1, 0, 2))
        return jnp.where(half_select, by_head[None], jnp.zeros_like(by_head)[None]).reshape(
            ctx_size, local_rows, per_head.shape[-1]
        )

    def gather_half(received):
        return lax.dynamic_slice_in_dim(received, my_half * half_devices, half_devices, 0).reshape(
            half_rows, received.shape[-1]
        )

    def from_heads(per_head):
        blocks = per_head.reshape(half_devices, local_rows, per_head.shape[-1])
        return jnp.where(half_select, blocks[None], jnp.zeros_like(blocks)[None]).reshape(
            ctx_size, local_rows, per_head.shape[-1]
        )

    def own_heads(received):
        mine = lax.dynamic_slice_in_dim(received, my_half * half_devices, half_devices, 0)
        return jnp.transpose(mine, (1, 0, 2))

    def exchange(values):
        return lax.all_to_all(values, CTX, split_axis=0, concat_axis=0, tiled=True)

    full_query, full_key, full_value, full_output, full_gate, full_up, full_down = (
        gather_fsdp(query_weight),
        gather_fsdp(key_projection),
        gather_fsdp(value_projection),
        gather_fsdp(output_weight),
        gather_fsdp(gate_weight),
        gather_fsdp(up_weight),
        gather_fsdp(down_weight),
    )
    input_f32 = layer_input[0].astype(jnp.float32)
    gained, first_normed, first_scale = rms_apply(input_f32, first_gain)
    attention_input = gained.astype(jnp.bfloat16)
    query_pre = jnp.dot(attention_input, full_query, preferred_element_type=jnp.float32).reshape(
        local_rows, HQ, HEAD_SIZE
    )
    query_gained, query_normed, query_scale = rms_apply(query_pre, query_gain)
    query_rotated = rotary_apply(query_gained, cosine_table, sine_values_table).astype(jnp.bfloat16)
    key_before_norm = jnp.dot(
        attention_input, full_key, preferred_element_type=jnp.float32
    ).reshape(local_rows, KEY_VALUE_HEADS, HEAD_SIZE)
    key_after_gain, key_after_norm, key_norm_scale = rms_apply(key_before_norm, key_norm_gain)
    own_keys = rotary_apply(key_after_gain, cosine_table, sine_values_table).astype(jnp.bfloat16)
    own_values = (
        jnp.dot(attention_input, full_value, preferred_element_type=jnp.float32)
        .astype(jnp.bfloat16)
        .reshape(local_rows, KEY_VALUE_HEADS, HEAD_SIZE)
    )
    group = HQ // KEY_VALUE_HEADS
    key_value = jnp.repeat(jnp.concatenate([own_keys, own_values], axis=-1), group, axis=1)
    sent = jnp.concatenate(
        [to_heads(query_rotated), jnp.tile(jnp.transpose(key_value, (1, 0, 2)), (halves, 1, 1))],
        axis=-1,
    )
    received = exchange(sent)
    head_query = gather_half(received[..., :HEAD_SIZE])
    head_key = received[..., HEAD_SIZE : 2 * HEAD_SIZE].reshape(-1, HEAD_SIZE)
    head_value = received[..., 2 * HEAD_SIZE :].reshape(-1, HEAD_SIZE)

    def head_scores():
        raw_scores = (
            jnp.einsum("qd,kd->qk", head_query, head_key, preferred_element_type=jnp.float32)
            * scale_factor
        )
        return jnp.where(allowed, raw_scores, MASKED)

    raw_scores = head_scores()
    row_max = jnp.max(raw_scores, axis=-1, keepdims=True)
    log_total = row_max + jnp.log(jnp.sum(jnp.exp(raw_scores - row_max), axis=-1, keepdims=True))
    weights_b = jnp.exp(raw_scores - log_total).astype(jnp.bfloat16)
    head_mixed = jnp.dot(weights_b, head_value, preferred_element_type=jnp.float32)
    mixed_b = own_heads(exchange(from_heads(head_mixed.astype(jnp.bfloat16)))).reshape(
        local_rows, HQ * HEAD_SIZE
    )
    residual_mid = input_f32 + jnp.dot(mixed_b, full_output, preferred_element_type=jnp.float32)
    gained_mid, second_normed, second_scale = rms_apply(residual_mid, second_gain)
    mlp_in = gained_mid.astype(jnp.bfloat16)
    gate_pre = jnp.dot(mlp_in, full_gate, preferred_element_type=jnp.float32)
    up_pre = jnp.dot(mlp_in, full_up, preferred_element_type=jnp.float32)
    sigmoid_gate = jax.nn.sigmoid(gate_pre)
    silu_gate = gate_pre * sigmoid_gate
    hidden = (silu_gate * up_pre).astype(jnp.bfloat16)
    layer_output = (
        residual_mid + jnp.dot(hidden, full_down, preferred_element_type=jnp.float32)
    ).astype(jnp.bfloat16)
    own_cotangent = cotangent[0]
    hidden_grad = right_dot(own_cotangent, full_down)
    gate_grad = (
        hidden_grad * up_pre * sigmoid_gate * (1.0 + gate_pre * (1.0 - sigmoid_gate))
    ).astype(jnp.bfloat16)
    up_grad = (hidden_grad * silu_gate).astype(jnp.bfloat16)
    mlp_in_grad = right_dot(gate_grad, full_gate) + right_dot(up_grad, full_up)
    second_gain_grad = jnp.sum(mlp_in_grad * second_normed, axis=0)
    mid_grad = own_cotangent.astype(jnp.float32) + root_mean_square_backward(
        mlp_in_grad, second_normed, second_scale, second_gain
    )
    mid_grad_b = mid_grad.astype(jnp.bfloat16)
    mixed_gradient = right_dot(mid_grad_b, full_output).astype(jnp.bfloat16)
    head_out_grad = gather_half(
        exchange(to_heads(mixed_gradient.reshape(local_rows, HQ, HEAD_SIZE)))
    )
    out_grad_f = head_out_grad.astype(jnp.float32)
    delta = jnp.sum(out_grad_f * head_mixed, axis=-1, keepdims=True)
    probabilities = jnp.exp(head_scores() - log_total)
    value_part = left_dot(probabilities.astype(jnp.bfloat16), head_out_grad)
    prob_grad = right_dot(head_out_grad, head_value)
    score_grad = (probabilities * (prob_grad - delta)).astype(jnp.bfloat16)
    query_part = jnp.dot(score_grad, head_key, preferred_element_type=jnp.float32) * scale_factor
    key_part = left_dot(score_grad, head_query) * scale_factor
    returned = exchange(
        jnp.concatenate(
            [
                from_heads(query_part.astype(jnp.bfloat16)),
                jnp.concatenate([key_part, value_part], axis=-1)
                .astype(jnp.bfloat16)
                .reshape(ctx_size, local_rows, 2 * HEAD_SIZE),
            ],
            axis=-1,
        )
    )
    query_grad_rows = own_heads(returned[..., :HEAD_SIZE]).astype(jnp.float32)
    kv_parts = (
        returned[..., HEAD_SIZE:]
        .astype(jnp.float32)
        .reshape(halves, KEY_VALUE_HEADS, group, local_rows, 2 * HEAD_SIZE)
    )
    kv_grad = jnp.transpose(jnp.sum(kv_parts, axis=(0, 2)), (1, 0, 2))
    local_key_gradient = kv_grad[..., :HEAD_SIZE]
    own_value_grad = kv_grad[..., HEAD_SIZE:].reshape(local_rows, KEY_VALUE_HEADS * HEAD_SIZE)
    query_back = rotary_backward(query_grad_rows, cosine_table, sine_values_table)
    query_gain_grad = jnp.sum(query_back * query_normed, axis=(0, 1))
    query_pre_grad = (
        root_mean_square_backward(query_back, query_normed, query_scale, query_gain)
        .astype(jnp.bfloat16)
        .reshape(local_rows, HQ * HEAD_SIZE)
    )
    key_backward_pass = rotary_backward(local_key_gradient, cosine_table, sine_values_table)
    key_gain_grad = jnp.sum(key_backward_pass * key_after_norm, axis=(0, 1))
    key_before_norm_gradient = (
        root_mean_square_backward(key_backward_pass, key_after_norm, key_norm_scale, key_norm_gain)
        .astype(jnp.bfloat16)
        .reshape(local_rows, KEY_VALUE_HEADS * HEAD_SIZE)
    )
    value_gradient_second = own_value_grad.astype(jnp.bfloat16)
    attn_in_grad = (
        right_dot(query_pre_grad, full_query)
        + right_dot(key_before_norm_gradient, full_key)
        + right_dot(value_gradient_second, full_value)
    )
    first_gain_grad = jnp.sum(attn_in_grad * first_normed, axis=0)
    input_grad = mid_grad + root_mean_square_backward(
        attn_in_grad, first_normed, first_scale, first_gain
    )
    attn_cols, mixed_cols, mlp_cols, hidden_cols = (
        lax.all_to_all(attention_input, FSDP, split_axis=1, concat_axis=0, tiled=True),
        lax.all_to_all(mixed_b, FSDP, split_axis=1, concat_axis=0, tiled=True),
        lax.all_to_all(mlp_in, FSDP, split_axis=1, concat_axis=0, tiled=True),
        lax.all_to_all(hidden, FSDP, split_axis=1, concat_axis=0, tiled=True),
    )
    cot_rows, gate_rows, up_rows, mid_rows, query_rows, key_rows, value_row_block = (
        gather_fsdp(own_cotangent),
        gather_fsdp(gate_grad),
        gather_fsdp(up_grad),
        gather_fsdp(mid_grad_b),
        gather_fsdp(query_pre_grad),
        gather_fsdp(key_before_norm_gradient),
        gather_fsdp(value_gradient_second),
    )
    query_shard = left_dot(attn_cols, query_rows)
    key_shard = left_dot(attn_cols, key_rows)
    value_shard = left_dot(attn_cols, value_row_block)
    output_shard = left_dot(mixed_cols, mid_rows)
    gate_shard = left_dot(mlp_cols, gate_rows)
    up_shard = left_dot(mlp_cols, up_rows)
    down_shard = left_dot(hidden_cols, cot_rows)
    first_shard, second_shard, query_gain_shard, key_gain_shard = (
        lax.psum_scatter(first_gain_grad, FSDP, scatter_dimension=0, tiled=True),
        lax.psum_scatter(second_gain_grad, FSDP, scatter_dimension=0, tiled=True),
        lax.psum_scatter(query_gain_grad, FSDP, scatter_dimension=0, tiled=True),
        lax.psum_scatter(key_gain_grad, FSDP, scatter_dimension=0, tiled=True),
    )
    shards = (
        query_shard,
        key_shard,
        value_shard,
        output_shard,
        gate_shard,
        up_shard,
        down_shard,
        first_shard,
        second_shard,
        query_gain_shard,
        key_gain_shard,
    )
    totals = reduce_ctx(shards)
    (
        query_total,
        key_total,
        value_total,
        output_total,
        gate_total,
        up_total,
        down_total,
        first_total,
        second_total,
        query_gain_total,
        key_gain_total,
    ) = totals
    return (
        layer_output[None],
        input_grad[None],
        query_total,
        key_total,
        value_total,
        output_total,
        gate_total,
        up_total,
        down_total,
        first_total,
        second_total,
        query_gain_total,
        key_gain_total,
    )


def solution(mesh):
    in_specs = (
        P(FSDP, CTX, None),
        P(FSDP, CTX, None),
        P(FSDP, None),
        P(FSDP, None),
        P(FSDP, None),
        P(FSDP, None),
        P(FSDP, None),
        P(FSDP, None),
        P(FSDP, None),
        P(FSDP, None),
        P(),
        P(),
        P(),
        P(),
    )
    out_specs = (
        P(FSDP, CTX, None),
        P(FSDP, CTX, None),
        P(FSDP, None),
        P(FSDP, None),
        P(FSDP, None),
        P(FSDP, None),
        P(FSDP, None),
        P(FSDP, None),
        P(FSDP, None),
        P(FSDP),
        P(FSDP),
        P(FSDP),
        P(FSDP),
    )
    torus_mesh = jax.sharding.Mesh(mesh.devices.reshape(2, 4, 4, 2, 2), ("yh", "x", "z", "yl", "c"))
    return jax.shard_map(
        on_device, mesh=torus_mesh, in_specs=in_specs, out_specs=out_specs, check_vma=False
    )
```

profile of v0, /device:TPU:1, one launch (start us, length us, event | category | flops | bytes accessed | tf_op | source)
XLA Modules:
  0.0 1240.5 jit_solution(9010868726562113697)
XLA Ops:
  11.2 25.6 %all-gather.61.cloned.1.call-done = bf16[512,1024]{1,0:T(8,128)(2,1)} async-done(((bf16[256,1024]{1,0:T(8,128)(2,1)}), bf16[512,1024]{1,0:T(8,128)(2,1)}) %all-gather.61.cloned.1.call-update) | async-done | bytes 1048592 | tf_op jit(solution)/shard_map/all_gather | solution.py:76
  36.8 26.4 %all-gather.65.cloned.1.call-done = bf16[512,1024]{1,0:T(8,128)(2,1)} async-done(((bf16[256,1024]{1,0:T(8,128)(2,1)}), bf16[512,1024]{1,0:T(8,128)(2,1)}) %all-gather.65.cloned.1.call-update) | async-done | bytes 1048592 | tf_op jit(solution)/shard_map/all_gather | solution.py:76
  63.3 38.2 %all-gather.57.cloned.1.call-done = bf16[512,2048]{1,0:T(8,128)(2,1)} async-done(((bf16[256,2048]{1,0:T(8,128)(2,1)}), bf16[512,2048]{1,0:T(8,128)(2,1)}) %all-gather.57.cloned.1.call-update) | async-done | bytes 2097168 | tf_op jit(solution)/shard_map/all_gather | solution.py:76
  102.2 37.5 %all-gather.69.cloned.1.call-done = bf16[1024,1024]{1,0:T(8,128)(2,1)} async-done(((bf16[512,1024]{1,0:T(8,128)(2,1)}), bf16[1024,1024]{1,0:T(8,128)(2,1)}) %all-gather.69.cloned.1.call-update) | async-done | bytes 2097168 | tf_op jit(solution)/shard_map/all_gather | solution.py:76
  139.8 49.9 %all-gather.73.cloned.1.call-done = bf16[512,3072]{1,0:T(8,128)(2,1)} async-done(((bf16[256,3072]{1,0:T(8,128)(2,1)}), bf16[512,3072]{1,0:T(8,128)(2,1)}) %all-gather.73.cloned.1.call-update) | async-done | bytes 3145744 | tf_op jit(solution)/shard_map/all_gather | solution.py:76
  190.3 49.3 %all-gather.77.cloned.1.call-done = bf16[512,3072]{1,0:T(8,128)(2,1)} async-done(((bf16[256,3072]{1,0:T(8,128)(2,1)}), bf16[512,3072]{1,0:T(8,128)(2,1)}) %all-gather.77.cloned.1.call-update) | async-done | bytes 3145744 | tf_op jit(solution)/shard_map/all_gather | solution.py:76
  239.9 16.1 %all-gather.63.cloned.1.call-done = bf16[2,512,1024]{2,1,0:T(8,128)(2,1)} async-done(((bf16[2,256,1024]{2,1,0:T(8,128)(2,1)}), bf16[2,512,1024]{2,1,0:T(8,128)(2,1)}) %all-gather.63.cloned.1.call-update) | async-done | bytes 2097168 | tf_op jit(solution)/shard_map/all_gather | solution.py:77
  278.2 13.5 %all-gather.59.cloned.1.call-done = bf16[2,512,2048]{2,1,0:T(8,128)(2,1)} async-done(((bf16[2,256,2048]{2,1,0:T(8,128)(2,1)}), bf16[2,512,2048]{2,1,0:T(8,128)(2,1)}) %all-gather.59.cloned.1.call-update) | async-done | bytes 4194320 | tf_op jit(solution)/shard_map/all_gather | solution.py:77
  319.2 56.7 %all-gather.81.cloned.1.call-done = bf16[1536,1024]{1,0:T(8,128)(2,1)} async-done(((bf16[768,1024]{1,0:T(8,128)(2,1)}), bf16[1536,1024]{1,0:T(8,128)(2,1)}) %all-gather.81.cloned.1.call-update) | async-done | bytes 3145744 | tf_op jit(solution)/shard_map/all_gather | solution.py:76
  378.2 14.4 %fusion.49 = (f32[2048]{0:T(1024)S(1)}, f32[2048,4096]{1,0:T(8,128)}) fusion(s32[2048]{0:T(1024)S(1)} %dynamic_slice.18, s32[4096]{0:T(1024)S(1)} %add.146, bf16[2048,128]{1,0:T(8,128)(2,1)S(1)} %bitcast.313, bf16[4096,128]{1,0:T(8,128)(2,1)S(1)} %bitcast.307), kind=kOutput, calls=%fused_computation.148 | convolution fusion | flops 2181036032 | bytes 35160064 | tf_op jit(solution)/shard_map/qd,kd->qk/dot_general | solution.py:199
  392.6 16.1 %exponential_reduce_fusion = f32[2048]{0:T(1024)S(1)} fusion(f32[2048]{0:T(1024)S(1)} %get-tuple-element.56, f32[2048,4096]{1,0:T(8,128)} %get-tuple-element.57, s32[2048]{0:T(1024)S(1)} %dynamic_slice.18, s32[4096]{0:T(1024)S(1)} %add.146), kind=kLoop, calls=%fused_computation.6 | loop fusion | flops 41940992 | bytes 33595392 | tf_op jit(solution)/shard_map/reduce_sum | solution.py:206
  408.7 18.5 %fusion.51 = (bf16[2048,128]{1,0:T(8,128)(2,1)S(1)}, f32[2048,128]{1,0:T(8,128)}) fusion(bf16[4096,128]{1,0:T(8,128)(2,1)S(1)} %bitcast.309, f32[2048]{0:T(1024)S(1)} %log_add_fusion, f32[2048,4096]{1,0:T(8,128)} %get-tuple-element.57, s32[2048]{0:T(1024)S(1)} %dynamic_slice.18, s32[4096]{0:T(1024)S(1)} %add.146), kind=kOutput, calls=%fused_computation.150 | convolution fusion | flops 2189688832 | bytes 36208640 | tf_op jit(solution)/shard_map/dot_general | solution.py:208
  427.6 28.8 %all_to_all.93 = bf16[32,128,128]{1,2,0:T(8,128)(2,1)S(1)} all-to-all(bf16[32,128,128]{1,2,0:T(8,128)(2,1)S(1)} %bitcast_select_fusion.3), channel_id=1, replica_groups=mesh['yh'=2,'x'=4,'z'=4,'yl'=2,'c'=2] {'yh','x','z'}, dimensions={0} | all-to-all | bytes 2097152 | tf_op jit(solution)/shard_map/all_to_all | solution.py:157
  503.5 20.3 %fusion.2 = bf16[4096,2048]{0,1:T(8,128)(2,1)} fusion(f32[2048,4096]{1,0:T(8,128)} %get-tuple-element.57, f32[2048]{0:T(1024)S(1)} %log_add_fusion, s32[4096]{0:T(1024)S(1)} %add.146, s32[2048]{0:T(1024)S(1)} %dynamic_slice.18), kind=kLoop, calls=%fused_computation.3 | loop fusion | flops 41943040 | bytes 50364416 | tf_op jit(solution)/shard_map/convert_element_type | solution.py:207
  523.8 22.6 %copy.81 = bf16[4096,2048]{1,0:T(8,128)(2,1)} copy(bf16[4096,2048]{0,1:T(8,128)(2,1)} %fusion.2) | data formatting | bytes 33554432 | tf_op jit(solution)/shard_map/dot_general | solution.py:64
  551.3 20.5 %multiply_convert_fusion = bf16[2048,4096]{1,0:T(8,128)(2,1)} fusion(f32[2048]{0:T(1024)S(1)} %multiply_reduce_fusion.2, f32[2048]{0:T(1024)S(1)} %log_add_fusion, bf16[2048,128]{1,0:T(8,128)(2,1)S(1)} %bitcast.265, bf16[4096,128]{1,0:T(8,128)(2,1)} %bitcast.310, f32[2048,4096]{1,0:T(8,128)} %get-tuple-element.57, s32[2048]{0:T(1024)S(1)} %dynamic_slice.18, ...), kind=kOutput, calls=%fused_computation.4 | convolution fusion | flops 2206203904 | bytes 51945472 | tf_op jit(solution)/shard_map/dot_general | solution.py:70
  618.4 44.4 %all_gather.212 = bf16[2,128,1024]{2,1,0:T(8,128)(2,1)} all-gather(bf16[1,128,1024]{2,1,0:T(8,128)(2,1)S(1)} %copy-done.15), channel_id=1, replica_groups=mesh['yh'=2,'x'=4,'z'=4,'yl'=2,'c'=2] {'yl'}, dimensions={0}, use_global_device_ids=true | all-gather | bytes 786432 | tf_op jit(solution)/shard_map/all_gather | solution.py:76
  702.2 22.3 %all_gather.197 = bf16[2,128,1024]{2,1,0:T(8,128)(2,1)} all-gather(bf16[1,128,1024]{2,1,0:T(8,128)(2,1)S(1)} %copy.74), channel_id=1, replica_groups=mesh['yh'=2,'x'=4,'z'=4,'yl'=2,'c'=2] {'yl'}, dimensions={0}, use_global_device_ids=true | all-gather | bytes 786432 | tf_op jit(solution)/shard_map/all_gather | solution.py:76
  832.0 103.5 %concatenate.38 = bf16[3932736]{0:T(1024)(128)(2,1)} concatenate(bf16[524288]{0:T(1024)(128)(2,1)} %bitcast.272, bf16[262144]{0:T(1024)(128)(2,1)} %bitcast.291, bf16[262144]{0:T(1024)(128)(2,1)} %bitcast.292, bf16[524288]{0:T(1024)(128)(2,1)S(1)} %bitcast.271, bf16[786432]{0:T(1024)(128)(2,1)} %bitcast.261, bf16[786432]{0:T(1024)(128)(2,1)} %bitcast.262, ...), dimensions={0} | concatenate | bytes 15730944 | tf_op jit(solution)/shard_map/concatenate | solution.py:82
  943.9 78.1 %reduce-scatter.3.cloned.1.call-done = bf16[7744,128]{1,0:T(8,128)(2,1)} async-done(((bf16[30976,128]{1,0:T(8,128)(2,1)}), bf16[7744,128]{1,0:T(8,128)(2,1)}) %reduce-scatter.3.cloned.1.call-update) | async-done | bytes 1982480 | tf_op jit(solution)/shard_map/reduce_scatter | solution.py:87
  1022.0 30.6 %reduce-scatter.5.cloned.1.call-done = bf16[1936,128]{1,0:T(8,128)(2,1)} async-done(((bf16[7744,128]{1,0:T(8,128)(2,1)}), bf16[1936,128]{1,0:T(8,128)(2,1)}) %reduce-scatter.5.cloned.1.call-update) | async-done | bytes 495632 | tf_op jit(solution)/shard_map/reduce_scatter | solution.py:88
  1052.7 37.9 %all-reduce.8.cloned.1.call-done = bf16[1936,128]{1,0:T(8,128)(2,1)} async-done(((bf16[1936,128]{1,0:T(8,128)(2,1)}), bf16[1936,128]{1,0:T(8,128)(2,1)}) %all-reduce.8.cloned.1.call-update) | async-done | bytes 495632 | tf_op jit(solution)/shard_map/psum | solution.py:89
  1091.0 31.0 %all-gather.53.cloned.1.call-done = bf16[7744,128]{1,0:T(8,128)(2,1)} async-done(((bf16[1936,128]{1,0:T(8,128)(2,1)}), bf16[7744,128]{1,0:T(8,128)(2,1)}) %all-gather.53.cloned.1.call-update) | async-done | bytes 1982480 | tf_op jit(solution)/shard_map/all_gather | solution.py:90
  1127.7 75.5 %all-gather.55.cloned.1.call-done = bf16[30976,128]{1,0:T(8,128)(2,1)} async-done(((bf16[7744,128]{1,0:T(8,128)(2,1)}), bf16[30976,128]{1,0:T(8,128)(2,1)}) %all-gather.55.cloned.1.call-update) | async-done | bytes 7929872 | tf_op jit(solution)/shard_map/all_gather | solution.py:91
  (295 shorter events, 346.1 us)
Async XLA Ops:
  8.7 92.9 %all-gather.57.cloned.1.call-start = ((), (), s32[]{:S(2)}) async-start(), calls=%async_computation.16 | async-start | bytes 3145728 | tf_op jit(solution)/shard_map/all_gather | solution.py:76
  9.4 130.3 %all-gather.69.cloned.1.call-start = ((), (), s32[]{:S(2)}) async-start(), calls=%async_computation.22 | async-start | bytes 3145728 | tf_op jit(solution)/shard_map/all_gather | solution.py:76
  10.0 179.7 %all-gather.73.cloned.1.call-start = ((), (), s32[]{:S(2)}) async-start(), calls=%async_computation.24 | async-start | bytes 4718592 | tf_op jit(solution)/shard_map/all_gather | solution.py:76
  10.6 229.1 %all-gather.77.cloned.1.call-start = ((), (), s32[]{:S(2)}) async-start(), calls=%async_computation.26 | async-start | bytes 4718592 | tf_op jit(solution)/shard_map/all_gather | solution.py:76
  11.1 244.9 %all-gather.63.cloned.1.call-start = ((), (), s32[]{:S(2)}) async-start(), calls=%async_computation.19 | async-start | bytes 3145728 | tf_op jit(solution)/shard_map/all_gather | solution.py:77
  36.8 235.6 %all-gather.67.cloned.1.call-start = ((), (), s32[]{:S(2)}) async-start(), calls=%async_computation.21 | async-start | bytes 3145728 | tf_op jit(solution)/shard_map/all_gather | solution.py:77
  63.3 228.5 %all-gather.59.cloned.1.call-start = ((), (), s32[]{:S(2)}) async-start(), calls=%async_computation.17 | async-start | bytes 6291456 | tf_op jit(solution)/shard_map/all_gather | solution.py:77
  101.6 274.4 %all-gather.81.cloned.1.call-start = ((), (), s32[]{:S(2)}) async-start(), calls=%async_computation.28 | async-start | bytes 4718592 | tf_op jit(solution)/shard_map/all_gather | solution.py:76
  102.2 354.4 %all-gather.71.cloned.1.call-start = ((), (), s32[]{:S(2)}) async-start(), calls=%async_computation.23 | async-start | bytes 6291456 | tf_op jit(solution)/shard_map/all_gather | solution.py:77
  139.7 320.7 %all-gather.75.cloned.1.call-start = ((), (), s32[]{:S(2)}) async-start(), calls=%async_computation.25 | async-start | bytes 9437184 | tf_op jit(solution)/shard_map/all_gather | solution.py:77
  189.7 276.7 %all-gather.79.cloned.1.call-start = ((), (), s32[]{:S(2)}) async-start(), calls=%async_computation.27 | async-start | bytes 9437184 | tf_op jit(solution)/shard_map/all_gather | solution.py:77
  318.9 152.4 %all-gather.83.cloned.1.call-start = ((), (), s32[]{:S(2)}) async-start(), calls=%async_computation.29 | async-start | bytes 9437184 | tf_op jit(solution)/shard_map/all_gather | solution.py:77
  503.1 175.5 %all-gather.93.cloned.1.call-start = ((), (), s32[]{:S(2)}) async-start(), calls=%async_computation.34 | async-start | bytes 2359296 | tf_op jit(solution)/shard_map/all_gather | solution.py:76
  618.3 117.1 %all-gather.101.cloned.1.call-start = ((), (), s32[]{:S(2)}) async-start(), calls=%async_computation.38 | async-start | bytes 1572864 | tf_op jit(solution)/shard_map/all_gather | solution.py:77
  662.8 76.7 %all-gather.51.cloned.1.call-start = ((), (), s32[]{:S(2)}) async-start(), calls=%async_computation.10 | async-start | bytes 1572864 | tf_op jit(solution)/shard_map/all_gather | solution.py:76
  668.0 79.1 %all-gather.91.cloned.1.call-start = ((), (), s32[]{:S(2)}) async-start(), calls=%async_computation.33 | async-start | bytes 1572864 | tf_op jit(solution)/shard_map/all_gather | solution.py:77
  678.5 91.6 %all-gather.95.cloned.1.call-start = ((), (), s32[]{:S(2)}) async-start(), calls=%async_computation.35 | async-start | bytes 4718592 | tf_op jit(solution)/shard_map/all_gather | solution.py:77
  679.1 103.6 %all-gather.99.cloned.1.call-start = ((), (), s32[]{:S(2)}) async-start(), calls=%async_computation.37 | async-start | bytes 4718592 | tf_op jit(solution)/shard_map/all_gather | solution.py:77
  679.8 117.6 %all-gather.87.cloned.1.call-start = ((), (), s32[]{:S(2)}) async-start(), calls=%async_computation.31 | async-start | bytes 1572864 | tf_op jit(solution)/shard_map/all_gather | solution.py:77
  701.0 111.2 %all-gather.89.cloned.1.call-start = ((), (), s32[]{:S(2)}) async-start(), calls=%async_computation.32 | async-start | bytes 1572864 | tf_op jit(solution)/shard_map/all_gather | solution.py:77
  731.9 96.5 %all-gather.85.cloned.1.call-start = ((), (), s32[]{:S(2)}) async-start(), calls=%async_computation.30 | async-start | bytes 3145728 | tf_op jit(solution)/shard_map/all_gather | solution.py:77
  770.1 251.9 %reduce-scatter.3.cloned.1.call-start = ((), (), s32[]{:S(2)}) async-start(), calls=%async_computation.11 | async-start | bytes 9912320 | tf_op jit(solution)/shard_map/reduce_scatter | solution.py:87
  943.8 108.8 %reduce-scatter.5.cloned.1.call-start = ((), (), s32[]{:S(2)}) async-start(), calls=%async_computation.12 | async-start | bytes 2478080 | tf_op jit(solution)/shard_map/reduce_scatter | solution.py:88
  1090.7 112.6 %all-gather.55.cloned.1.call-start = ((), (), s32[]{:S(2)}) async-start(), calls=%async_computation.15 | async-start | bytes 9912320 | tf_op jit(solution)/shard_map/all_gather | solution.py:91
  (52 other events, 1499.4 us)
Sparse Core Ops, SparseCore 0:
  9.7 27.0 all-gather.60
  38.4 24.7 all-gather.64
  64.9 36.6 all-gather.56
  103.0 36.6 all-gather.68
  141.2 48.4 all-gather.72
  191.2 48.4 all-gather.76
  274.0 17.6 all-gather.58
  293.2 82.6 all-gather.80
  377.6 21.7 all-gather.70
  400.9 20.8 all-gather.74
  423.4 20.7 all-gather.78
  445.7 20.7 all-gather.82
  546.6 31.9 all-gather.92
  620.5 57.1 all-gather.96
  679.2 15.1 all-gather.100
  696.5 32.6 all-gather.50
  730.9 16.0 all-gather.90
  748.5 16.2 all-gather.94
  766.5 16.1 all-gather.98
  944.0 77.9 reduce-scatter.2
  1024.2 28.3 reduce-scatter.4
  1055.1 35.4 all-reduce.7
  1092.4 29.5 all-gather.52
  1123.7 79.5 all-gather.54
  (5 shorter events, 69.7 us)
where the time goes:
time: 1260 us; the launch traced here: 1240 us
  waiting for transfers between devices  631 us (50%)
  local copies, waits for them, and re-layouts  204 us (16%)
  matrix products  146 us (12%)
  blocking collectives  122 us (10%)
  other arithmetic  69.1 us (5%)
  starting transfers between devices  51.6 us (4%)
  between operations  16.7 us (1%)
    all_gather x10, waiting for transfers between devices, gather_fsdp(): across = lax.all_gather(values, 'yl', axis=0, tiled=False)  284 us
    concatenate x1, local copies, waits for them, and re-layouts, reduce_ctx(): flat = jnp.concatenate([s.astype(jnp.bfloat16).reshape(-1) for s in shards])  104 us
    all_gather x14, waiting for transfers between devices, gather_fsdp(): both = lax.all_gather(across, 'c', axis=1, tiled=False)  87.8 us
    all_gather x4, blocking collectives, gather_fsdp(): across = lax.all_gather(values, 'yl', axis=0, tiled=False)  83.6 us
    reduce_scatter x1, waiting for transfers between devices, reduce_ctx(): part = lax.psum_scatter(flat, 'z', scatter_dimension=0, tiled=True)  78.1 us
    all_gather x1, waiting for transfers between devices, reduce_ctx(): full = lax.all_gather(part, 'z', axis=0, tiled=True).reshape(-1)  75.5 us
    dot_general x8, matrix products, right_dot(): lax.dot_general(left_side, right_side, (((1,), (1,)), ((), ())), preferre...  45.2 us
    psum x1, waiting for transfers between devices, reduce_ctx(): part = lax.psum(part, 'yh')  37.9 us
  transfers between devices with their start and end apart: 36, of which 21 were waited for; matrix products, arithmetic and copies ran while one was open for 20% of the time, Pallas kernels for 0%

commit v1 on v0

--- a/solution.py
+++ b/solution.py
@@ -86,7 +86,7 @@
     flat = jnp.pad(flat, (0, padded - flat.shape[0])).reshape(padded // lanes, lanes)
     part = lax.psum_scatter(flat, "z", scatter_dimension=0, tiled=True)
     part = lax.psum_scatter(part, "x", scatter_dimension=0, tiled=True)
-    part = lax.psum(part, "yh")
+    part = jnp.sum(lax.all_gather(part, "yh"), axis=0)
     part = lax.all_gather(part, "x", axis=0, tiled=True)
     full = lax.all_gather(part, "z", axis=0, tiled=True).reshape(-1)
     out = []

time: 1260 us -> 1240 us (0.984)
  waiting for transfers between devices: 631 us -> 592 us
  blocking collectives: 122 us -> 137 us
    psum x1 -> x0, waiting for transfers between devices: 37.9 us -> none  [reduce_ctx(): part = lax.psum(part, 'yh')]
    all_gather x0 -> x1, blocking collectives: none -> 14.6 us  [reduce_ctx(): part = jnp.sum(lax.all_gather(part, 'yh'), axis=0)]
  transfers between devices with their start and end apart: 36 -> 35, of which waited for: 21 -> 20; matrix products, arithmetic and copies ran while one was open for 20% -> 20% of each run, Pallas kernels for 0% -> 0%
where the time goes in v1:
time: 1240 us; the launch traced here: 1220 us
  waiting for transfers between devices  592 us (48%)
  local copies, waits for them, and re-layouts  205 us (17%)
  matrix products  146 us (12%)
  blocking collectives  137 us (11%)
  other arithmetic  70.1 us (6%)
  starting transfers between devices  51.4 us (4%)
  between operations  17 us (1%)
    all_gather x10, waiting for transfers between devices, gather_fsdp(): across = lax.all_gather(values, 'yl', axis=0, tiled=False)  284 us
    concatenate x1, local copies, waits for them, and re-layouts, reduce_ctx(): flat = jnp.concatenate([s.astype(jnp.bfloat16).reshape(-1) for s in shards])  104 us
    all_gather x14, waiting for transfers between devices, gather_fsdp(): both = lax.all_gather(across, 'c', axis=1, tiled=False)  87.8 us
    all_gather x4, blocking collectives, gather_fsdp(): across = lax.all_gather(values, 'yl', axis=0, tiled=False)  83.7 us
    reduce_scatter x1, waiting for transfers between devices, reduce_ctx(): part = lax.psum_scatter(flat, 'z', scatter_dimension=0, tiled=True)  78.1 us
    all_gather x1, waiting for transfers between devices, reduce_ctx(): full = lax.all_gather(part, 'z', axis=0, tiled=True).reshape(-1)  75.5 us
    dot_general x8, matrix products, right_dot(): lax.dot_general(left_side, right_side, (((1,), (1,)), ((), ())), preferre...  45.2 us
    dot_general x9, matrix products, left_dot(): lax.dot_general(left_side, right_side, (((0,), (0,)), ((), ())), preferre...  32.7 us
  transfers between devices with their start and end apart: 35, of which 20 were waited for; matrix products, arithmetic and copies ran while one was open for 20% of the time, Pallas kernels for 0%

profile of v1, /device:TPU:1, one launch (start us, length us, event | category | flops | bytes accessed | tf_op | source)
XLA Modules:
  0.0 1218.6 jit_solution(5021884124889565979)
XLA Ops:
  11.2 25.6 %all-gather.62.cloned.1.call-done = bf16[512,1024]{1,0:T(8,128)(2,1)} async-done(((bf16[256,1024]{1,0:T(8,128)(2,1)}), bf16[512,1024]{1,0:T(8,128)(2,1)}) %all-gather.62.cloned.1.call-update) | async-done | bytes 1048592 | tf_op jit(solution)/shard_map/all_gather | solution.py:76
  36.8 26.4 %all-gather.66.cloned.1.call-done = bf16[512,1024]{1,0:T(8,128)(2,1)} async-done(((bf16[256,1024]{1,0:T(8,128)(2,1)}), bf16[512,1024]{1,0:T(8,128)(2,1)}) %all-gather.66.cloned.1.call-update) | async-done | bytes 1048592 | tf_op jit(solution)/shard_map/all_gather | solution.py:76
  63.3 38.2 %all-gather.58.cloned.1.call-done = bf16[512,2048]{1,0:T(8,128)(2,1)} async-done(((bf16[256,2048]{1,0:T(8,128)(2,1)}), bf16[512,2048]{1,0:T(8,128)(2,1)}) %all-gather.58.cloned.1.call-update) | async-done | bytes 2097168 | tf_op jit(solution)/shard_map/all_gather | solution.py:76
  102.2 37.5 %all-gather.70.cloned.1.call-done = bf16[1024,1024]{1,0:T(8,128)(2,1)} async-done(((bf16[512,1024]{1,0:T(8,128)(2,1)}), bf16[1024,1024]{1,0:T(8,128)(2,1)}) %all-gather.70.cloned.1.call-update) | async-done | bytes 2097168 | tf_op jit(solution)/shard_map/all_gather | solution.py:76
  139.8 49.9 %all-gather.74.cloned.1.call-done = bf16[512,3072]{1,0:T(8,128)(2,1)} async-done(((bf16[256,3072]{1,0:T(8,128)(2,1)}), bf16[512,3072]{1,0:T(8,128)(2,1)}) %all-gather.74.cloned.1.call-update) | async-done | bytes 3145744 | tf_op jit(solution)/shard_map/all_gather | solution.py:76
  190.3 49.3 %all-gather.78.cloned.1.call-done = bf16[512,3072]{1,0:T(8,128)(2,1)} async-done(((bf16[256,3072]{1,0:T(8,128)(2,1)}), bf16[512,3072]{1,0:T(8,128)(2,1)}) %all-gather.78.cloned.1.call-update) | async-done | bytes 3145744 | tf_op jit(solution)/shard_map/all_gather | solution.py:76
  239.9 16.1 %all-gather.64.cloned.1.call-done = bf16[2,512,1024]{2,1,0:T(8,128)(2,1)} async-done(((bf16[2,256,1024]{2,1,0:T(8,128)(2,1)}), bf16[2,512,1024]{2,1,0:T(8,128)(2,1)}) %all-gather.64.cloned.1.call-update) | async-done | bytes 2097168 | tf_op jit(solution)/shard_map/all_gather | solution.py:77
  278.2 13.5 %all-gather.60.cloned.1.call-done = bf16[2,512,2048]{2,1,0:T(8,128)(2,1)} async-done(((bf16[2,256,2048]{2,1,0:T(8,128)(2,1)}), bf16[2,512,2048]{2,1,0:T(8,128)(2,1)}) %all-gather.60.cloned.1.call-update) | async-done | bytes 4194320 | tf_op jit(solution)/shard_map/all_gather | solution.py:77
  319.2 56.7 %all-gather.82.cloned.1.call-done = bf16[1536,1024]{1,0:T(8,128)(2,1)} async-done(((bf16[768,1024]{1,0:T(8,128)(2,1)}), bf16[1536,1024]{1,0:T(8,128)(2,1)}) %all-gather.82.cloned.1.call-update) | async-done | bytes 3145744 | tf_op jit(solution)/shard_map/all_gather | solution.py:76
  378.1 14.4 %fusion.49 = (f32[2048]{0:T(1024)S(1)}, f32[2048,4096]{1,0:T(8,128)}) fusion(s32[2048]{0:T(1024)S(1)} %dynamic_slice.18, s32[4096]{0:T(1024)S(1)} %add.144, bf16[2048,128]{1,0:T(8,128)(2,1)S(1)} %bitcast.315, bf16[4096,128]{1,0:T(8,128)(2,1)S(1)} %bitcast.309), kind=kOutput, calls=%fused_computation.148 | convolution fusion | flops 2181036032 | bytes 35160064 | tf_op jit(solution)/shard_map/qd,kd->qk/dot_general | solution.py:199
  392.5 16.1 %exponential_reduce_fusion = f32[2048]{0:T(1024)S(1)} fusion(f32[2048]{0:T(1024)S(1)} %get-tuple-element.56, f32[2048,4096]{1,0:T(8,128)} %get-tuple-element.57, s32[2048]{0:T(1024)S(1)} %dynamic_slice.18, s32[4096]{0:T(1024)S(1)} %add.144), kind=kLoop, calls=%fused_computation.6 | loop fusion | flops 41940992 | bytes 33595392 | tf_op jit(solution)/shard_map/reduce_sum | solution.py:206
  408.6 18.5 %fusion.51 = (bf16[2048,128]{1,0:T(8,128)(2,1)S(1)}, f32[2048,128]{1,0:T(8,128)}) fusion(bf16[4096,128]{1,0:T(8,128)(2,1)S(1)} %bitcast.311, f32[2048]{0:T(1024)S(1)} %log_add_fusion, f32[2048,4096]{1,0:T(8,128)} %get-tuple-element.57, s32[2048]{0:T(1024)S(1)} %dynamic_slice.18, s32[4096]{0:T(1024)S(1)} %add.144), kind=kOutput, calls=%fused_computation.150 | convolution fusion | flops 2189688832 | bytes 36208640 | tf_op jit(solution)/shard_map/dot_general | solution.py:208
  427.5 29.0 %all_to_all.93 = bf16[32,128,128]{1,2,0:T(8,128)(2,1)S(1)} all-to-all(bf16[32,128,128]{1,2,0:T(8,128)(2,1)S(1)} %bitcast_select_fusion.3), channel_id=1, replica_groups=mesh['yh'=2,'x'=4,'z'=4,'yl'=2,'c'=2] {'yh','x','z'}, dimensions={0} | all-to-all | bytes 2097152 | tf_op jit(solution)/shard_map/all_to_all | solution.py:157
  503.5 20.3 %fusion.2 = bf16[4096,2048]{0,1:T(8,128)(2,1)} fusion(f32[2048,4096]{1,0:T(8,128)} %get-tuple-element.57, f32[2048]{0:T(1024)S(1)} %log_add_fusion, s32[4096]{0:T(1024)S(1)} %add.144, s32[2048]{0:T(1024)S(1)} %dynamic_slice.18), kind=kLoop, calls=%fused_computation.3 | loop fusion | flops 41943040 | bytes 50364416 | tf_op jit(solution)/shard_map/convert_element_type | solution.py:207
  523.8 22.5 %copy.101 = bf16[4096,2048]{1,0:T(8,128)(2,1)} copy(bf16[4096,2048]{0,1:T(8,128)(2,1)} %fusion.2) | data formatting | bytes 33554432 | tf_op jit(solution)/shard_map/dot_general | solution.py:64
  551.2 20.5 %multiply_convert_fusion = bf16[2048,4096]{1,0:T(8,128)(2,1)} fusion(f32[2048]{0:T(1024)S(1)} %multiply_reduce_fusion.2, f32[2048]{0:T(1024)S(1)} %log_add_fusion, bf16[2048,128]{1,0:T(8,128)(2,1)S(1)} %bitcast.266, bf16[4096,128]{1,0:T(8,128)(2,1)} %bitcast.312, f32[2048,4096]{1,0:T(8,128)} %get-tuple-element.57, s32[2048]{0:T(1024)S(1)} %dynamic_slice.18, ...), kind=kOutput, calls=%fused_computation.4 | convolution fusion | flops 2206203904 | bytes 51945472 | tf_op jit(solution)/shard_map/dot_general | solution.py:70
  618.3 44.4 %all_gather.218 = bf16[2,128,1024]{2,1,0:T(8,128)(2,1)} all-gather(bf16[1,128,1024]{2,1,0:T(8,128)(2,1)S(1)} %copy-done.15), channel_id=1, replica_groups=mesh['yh'=2,'x'=4,'z'=4,'yl'=2,'c'=2] {'yl'}, dimensions={0}, use_global_device_ids=true | all-gather | bytes 786432 | tf_op jit(solution)/shard_map/all_gather | solution.py:76
  702.2 22.4 %all_gather.203 = bf16[2,128,1024]{2,1,0:T(8,128)(2,1)} all-gather(bf16[1,128,1024]{2,1,0:T(8,128)(2,1)S(1)} %copy.94), channel_id=1, replica_groups=mesh['yh'=2,'x'=4,'z'=4,'yl'=2,'c'=2] {'yl'}, dimensions={0}, use_global_device_ids=true | all-gather | bytes 786432 | tf_op jit(solution)/shard_map/all_gather | solution.py:76
  831.9 104.4 %concatenate.38 = bf16[3932736]{0:T(1024)(128)(2,1)} concatenate(bf16[524288]{0:T(1024)(128)(2,1)} %bitcast.273, bf16[262144]{0:T(1024)(128)(2,1)} %bitcast.293, bf16[262144]{0:T(1024)(128)(2,1)} %bitcast.294, bf16[524288]{0:T(1024)(128)(2,1)S(1)} %bitcast.272, bf16[786432]{0:T(1024)(128)(2,1)} %bitcast.262, bf16[786432]{0:T(1024)(128)(2,1)} %bitcast.263, ...), dimensions={0} | concatenate | bytes 15730944 | tf_op jit(solution)/shard_map/concatenate | solution.py:82
  944.7 78.1 %reduce-scatter.3.cloned.1.call-done = bf16[7744,128]{1,0:T(8,128)(2,1)} async-done(((bf16[30976,128]{1,0:T(8,128)(2,1)}), bf16[7744,128]{1,0:T(8,128)(2,1)}) %reduce-scatter.3.cloned.1.call-update) | async-done | bytes 1982480 | tf_op jit(solution)/shard_map/reduce_scatter | solution.py:87
  1022.8 30.6 %reduce-scatter.5.cloned.1.call-done = bf16[1936,128]{1,0:T(8,128)(2,1)} async-done(((bf16[7744,128]{1,0:T(8,128)(2,1)}), bf16[1936,128]{1,0:T(8,128)(2,1)}) %reduce-scatter.5.cloned.1.call-update) | async-done | bytes 495632 | tf_op jit(solution)/shard_map/reduce_scatter | solution.py:88
  1053.4 14.6 %all-gather.24 = bf16[3872,128]{1,0:T(8,128)(2,1)S(1)} all-gather(bf16[1936,128]{1,0:T(8,128)(2,1)} %reduce-scatter.5.cloned.1.call-done), channel_id=26, replica_groups=mesh['yh'=2,'x'=4,'z'=4,'yl'=2,'c'=2] {'yh'}, dimensions={0}, use_global_device_ids=true | all-gather | bytes 1486848 | tf_op jit(solution)/shard_map/all_gather | solution.py:89
  1069.4 30.3 %all-gather.54.cloned.1.call-done = bf16[7744,128]{1,0:T(8,128)(2,1)} async-done(((bf16[1936,128]{1,0:T(8,128)(2,1)}), bf16[7744,128]{1,0:T(8,128)(2,1)}) %all-gather.54.cloned.1.call-update) | async-done | bytes 1982480 | tf_op jit(solution)/shard_map/all_gather | solution.py:90
  1105.5 75.5 %all-gather.56.cloned.1.call-done = bf16[30976,128]{1,0:T(8,128)(2,1)} async-done(((bf16[7744,128]{1,0:T(8,128)(2,1)}), bf16[30976,128]{1,0:T(8,128)(2,1)}) %all-gather.56.cloned.1.call-update) | async-done | bytes 7929872 | tf_op jit(solution)/shard_map/all_gather | solution.py:91
  (294 shorter events, 347.0 us)
Async XLA Ops:
  8.7 92.9 %all-gather.58.cloned.1.call-start = ((), (), s32[]{:S(2)}) async-start(), calls=%async_computation.15 | async-start | bytes 3145728 | tf_op jit(solution)/shard_map/all_gather | solution.py:76
  9.4 130.3 %all-gather.70.cloned.1.call-start = ((), (), s32[]{:S(2)}) async-start(), calls=%async_computation.21 | async-start | bytes 3145728 | tf_op jit(solution)/shard_map/all_gather | solution.py:76
  10.0 179.7 %all-gather.74.cloned.1.call-start = ((), (), s32[]{:S(2)}) async-start(), calls=%async_computation.23 | async-start | bytes 4718592 | tf_op jit(solution)/shard_map/all_gather | solution.py:76
  10.6 229.1 %all-gather.78.cloned.1.call-start = ((), (), s32[]{:S(2)}) async-start(), calls=%async_computation.25 | async-start | bytes 4718592 | tf_op jit(solution)/shard_map/all_gather | solution.py:76
  11.1 244.9 %all-gather.64.cloned.1.call-start = ((), (), s32[]{:S(2)}) async-start(), calls=%async_computation.18 | async-start | bytes 3145728 | tf_op jit(solution)/shard_map/all_gather | solution.py:77
  36.8 235.6 %all-gather.68.cloned.1.call-start = ((), (), s32[]{:S(2)}) async-start(), calls=%async_computation.20 | async-start | bytes 3145728 | tf_op jit(solution)/shard_map/all_gather | solution.py:77
  63.3 228.5 %all-gather.60.cloned.1.call-start = ((), (), s32[]{:S(2)}) async-start(), calls=%async_computation.16 | async-start | bytes 6291456 | tf_op jit(solution)/shard_map/all_gather | solution.py:77
  101.6 274.3 %all-gather.82.cloned.1.call-start = ((), (), s32[]{:S(2)}) async-start(), calls=%async_computation.27 | async-start | bytes 4718592 | tf_op jit(solution)/shard_map/all_gather | solution.py:76
  102.2 354.4 %all-gather.72.cloned.1.call-start = ((), (), s32[]{:S(2)}) async-start(), calls=%async_computation.22 | async-start | bytes 6291456 | tf_op jit(solution)/shard_map/all_gather | solution.py:77
  139.7 320.7 %all-gather.76.cloned.1.call-start = ((), (), s32[]{:S(2)}) async-start(), calls=%async_computation.24 | async-start | bytes 9437184 | tf_op jit(solution)/shard_map/all_gather | solution.py:77
  189.7 276.7 %all-gather.80.cloned.1.call-start = ((), (), s32[]{:S(2)}) async-start(), calls=%async_computation.26 | async-start | bytes 9437184 | tf_op jit(solution)/shard_map/all_gather | solution.py:77
  318.9 152.4 %all-gather.84.cloned.1.call-start = ((), (), s32[]{:S(2)}) async-start(), calls=%async_computation.28 | async-start | bytes 9437184 | tf_op jit(solution)/shard_map/all_gather | solution.py:77
  503.1 175.4 %all-gather.94.cloned.1.call-start = ((), (), s32[]{:S(2)}) async-start(), calls=%async_computation.33 | async-start | bytes 2359296 | tf_op jit(solution)/shard_map/all_gather | solution.py:76
  618.3 117.1 %all-gather.102.cloned.1.call-start = ((), (), s32[]{:S(2)}) async-start(), calls=%async_computation.37 | async-start | bytes 1572864 | tf_op jit(solution)/shard_map/all_gather | solution.py:77
  667.9 79.1 %all-gather.92.cloned.1.call-start = ((), (), s32[]{:S(2)}) async-start(), calls=%async_computation.32 | async-start | bytes 1572864 | tf_op jit(solution)/shard_map/all_gather | solution.py:77
  678.4 91.6 %all-gather.96.cloned.1.call-start = ((), (), s32[]{:S(2)}) async-start(), calls=%async_computation.34 | async-start | bytes 4718592 | tf_op jit(solution)/shard_map/all_gather | solution.py:77
  679.0 103.6 %all-gather.100.cloned.1.call-start = ((), (), s32[]{:S(2)}) async-start(), calls=%async_computation.36 | async-start | bytes 4718592 | tf_op jit(solution)/shard_map/all_gather | solution.py:77
  679.8 117.6 %all-gather.88.cloned.1.call-start = ((), (), s32[]{:S(2)}) async-start(), calls=%async_computation.30 | async-start | bytes 1572864 | tf_op jit(solution)/shard_map/all_gather | solution.py:77
  700.9 111.2 %all-gather.90.cloned.1.call-start = ((), (), s32[]{:S(2)}) async-start(), calls=%async_computation.31 | async-start | bytes 1572864 | tf_op jit(solution)/shard_map/all_gather | solution.py:77
  731.9 96.4 %all-gather.86.cloned.1.call-start = ((), (), s32[]{:S(2)}) async-start(), calls=%async_computation.29 | async-start | bytes 3145728 | tf_op jit(solution)/shard_map/all_gather | solution.py:77
  770.0 252.7 %reduce-scatter.3.cloned.1.call-start = ((), (), s32[]{:S(2)}) async-start(), calls=%async_computation.11 | async-start | bytes 9912320 | tf_op jit(solution)/shard_map/reduce_scatter | solution.py:87
  944.6 108.8 %reduce-scatter.5.cloned.1.call-start = ((), (), s32[]{:S(2)}) async-start(), calls=%async_computation.12 | async-start | bytes 2478080 | tf_op jit(solution)/shard_map/reduce_scatter | solution.py:88
  1022.7 77.0 %all-gather.54.cloned.1.call-start = ((), (), s32[]{:S(2)}) async-start(), calls=%async_computation.13 | async-start | bytes 2478080 | tf_op jit(solution)/shard_map/all_gather | solution.py:90
  1069.1 111.9 %all-gather.56.cloned.1.call-start = ((), (), s32[]{:S(2)}) async-start(), calls=%async_computation.14 | async-start | bytes 9912320 | tf_op jit(solution)/shard_map/all_gather | solution.py:91
  (51 other events, 1415.3 us)
Sparse Core Ops, SparseCore 0:
  9.7 27.0 all-gather.61
  38.4 24.7 all-gather.65
  64.9 36.6 all-gather.57
  103.0 36.6 all-gather.69
  141.2 48.4 all-gather.73
  191.2 48.4 all-gather.77
  241.3 14.6 all-gather.63
  274.0 17.6 all-gather.59
  293.2 82.5 all-gather.81
  377.5 21.7 all-gather.71
  400.8 20.8 all-gather.75
  423.4 20.7 all-gather.79
  445.7 20.7 all-gather.83
  546.5 31.9 all-gather.93
  620.4 57.1 all-gather.97
  679.2 15.1 all-gather.101
  696.5 32.7 all-gather.51
  730.9 16.0 all-gather.91
  748.5 16.2 all-gather.95
  766.4 16.1 all-gather.99
  944.7 77.9 reduce-scatter.2
  1025.0 28.3 reduce-scatter.4
  1069.2 30.4 all-gather.53
  1101.5 79.5 all-gather.55
  (4 shorter events, 55.1 us)
